TPU v7x, 32 devices: a whole 2x2x4 slice. The times are simulated.
32 devices in a mesh: dp: 4 (over y, core), item: 8 (over z, x).
Axes of the slice: x: 2, y: 2, z: 4, core: 2. Of those that a mesh axis runs over, the one named last changes fastest.
Arguments:
- query: bfloat16 [32, 256], P(('dp', 'item')), may hold values from -40 to 40
- item_table: bfloat16 [65536, 256], P(('dp', 'item')), may hold values from -2.5 to 2.5
- context_features: bfloat16 [32, 512], P(('dp', 'item')), may hold values from -6 to 6
- candidates: int32 [32, 1024], P(('dp', 'item')), may hold values from 0 to 65535, as said below
- lengths: int32 [32], P(('dp', 'item')), may hold values from 128 to 1024, as said below
- logged_slot: int32 [32], P(('dp', 'item')), may hold values from 0 to 1023, as said below
- logging_prop: int32 [32], P(('dp', 'item')), may hold values from 256 to 4095
- w_first: bfloat16 [768, 512], replicated, may hold values from -0.21875 to 0.21875
- w_second: bfloat16 [512, 512], replicated, may hold values from -0.25 to 0.25
- w_score: bfloat16 [512], replicated, may hold values from -0.5 to 0.5
Outputs:
- section_logp: float32 [32, 1024], P(('dp', 'item'))
- log_weight: float32 [32], P(('dp', 'item'))
Inputs may be any that keep to these rules, and one draw needn't show every extreme that they name: `candidates`: item ids. Among the 1024 candidate slots held by one device (its single context), at most 48 name items of any one block of 2048 consecutive ids, and for every device some block is named exactly 48 times. `lengths`: some context's list has 1024 live slots and some context's list has 128. `logged_slot`: below the context's length; the context with the longest list logs its last slot.
All inputs are finite; a program needn't handle non-finite values.
Results may differ from a plain program's by a relative error of at most 0.0003.
Values may be sent and summed in bfloat16 or wider, within the bound.
A program may use at most 64 MiB of HBM per device.

v0:
```python
import math
import jax
import jax.numpy as jnp
from jax import lax
from jax.sharding import PartitionSpec as P


def merged(array, axis, combine):
    everything = jax.tree.map(lambda part: lax.all_gather(part, axis), array)
    leading = jax.tree.map(lambda part: part[0], everything)

    def step(k, so_far):
        return combine(so_far, jax.tree.map(lambda part: part[k], everything))

    return lax.fori_loop(1, lax.axis_size(axis), step, leading)


def combine_pairs(earlier, later):
    new_max = jnp.maximum(earlier[0], later[0])
    new_sum = earlier[1] * jnp.exp(earlier[0] - new_max) + later[1] * jnp.exp(later[0] - new_max)
    return (new_max, new_sum)


def body(
    query,
    item_table,
    context_features,
    candidates,
    lengths,
    logged_slot,
    logging_prop,
    w_first,
    w_second,
    w_score,
):
    device_count = lax.axis_size("dp") * lax.axis_size("item")
    item_rows = item_table.shape[0]
    width = item_table.shape[1]
    own_count = query.shape[0]
    slot_count = candidates.shape[1]
    gathered = lax.all_gather(query, ("dp", "item"), axis=0, tiled=True)
    context_total = gathered.shape[0]
    block_rows = min(512, item_rows)
    slabs = item_table.reshape(item_rows // block_rows, block_rows, width)

    def sweep(running, slab_rows):
        running_max, running_sum = running
        logits = lax.dot_general(
            gathered, slab_rows, (((1,), (1,)), ((), ())), preferred_element_type=jnp.float32
        )
        new_max = jnp.maximum(running_max, jnp.max(logits, axis=1))
        new_sum = running_sum * jnp.exp(running_max - new_max) + jnp.sum(
            jnp.exp(logits - new_max[:, None]), axis=1
        )
        return ((new_max, new_sum), None)

    initial = (
        jnp.full((context_total,), -1e30, jnp.float32),
        jnp.zeros((context_total,), jnp.float32),
    )
    (local_max, local_sum), unused_out = lax.scan(sweep, initial, slabs)
    first_context = lax.axis_index(("dp", "item")) * own_count
    global_max, global_sum = merged((local_max, local_sum), ("dp", "item"), combine_pairs)
    log_norm = lax.dynamic_slice_in_dim(global_max + jnp.log(global_sum), first_context, own_count)
    capacity = max(2, 3 * own_count * slot_count // (2 * device_count))
    flat_ids = candidates.reshape(-1)
    holder = flat_ids // item_rows
    same_holder = holder[:, None] == holder[None, :]
    earlier_slot = jnp.arange(flat_ids.shape[0])[None, :] < jnp.arange(flat_ids.shape[0])[:, None]
    holder_rank = jnp.sum((same_holder & earlier_slot).astype(jnp.int32), axis=1)
    bucket = holder * capacity + holder_rank
    outgoing = jnp.full((device_count * capacity,), -1, jnp.int32).at[bucket].set(flat_ids)
    outgoing = outgoing.reshape(lax.axis_size("dp"), lax.axis_size("item"), capacity)
    first_item = lax.axis_index(("dp", "item")) * item_rows
    asked_ids = lax.all_to_all(
        lax.all_to_all(outgoing, "dp", split_axis=0, concat_axis=0, tiled=True),
        "item",
        split_axis=1,
        concat_axis=1,
        tiled=True,
    )
    local_index = jnp.clip(asked_ids - first_item, 0, item_rows - 1)
    fetched = lax.all_to_all(
        lax.all_to_all(item_table[local_index], "dp", split_axis=0, concat_axis=0, tiled=True),
        "item",
        split_axis=1,
        concat_axis=1,
        tiled=True,
    )
    cand_rows = fetched.reshape(device_count * capacity, width)[bucket]
    rows_by_context = cand_rows.reshape(own_count, slot_count, width)
    gen_logit = jnp.einsum("cd,ckd->ck", query, rows_by_context, preferred_element_type=jnp.float32)
    feature_width = context_features.shape[1]
    context_part = jnp.dot(
        context_features, w_first[:feature_width], preferred_element_type=jnp.float32
    )
    item_part = jnp.dot(cand_rows, w_first[feature_width:], preferred_element_type=jnp.float32)
    item_part = item_part.reshape(own_count, slot_count, -1)
    hidden = jax.nn.silu(item_part + context_part[:, None, :]).astype(jnp.bfloat16)
    hidden = hidden.reshape(own_count * slot_count, -1)
    second = jax.nn.silu(jnp.dot(hidden, w_second, preferred_element_type=jnp.float32)).astype(
        jnp.bfloat16
    )
    score = jnp.dot(second, w_score, preferred_element_type=jnp.float32).reshape(
        own_count, slot_count
    )
    positions = jnp.arange(slot_count, dtype=jnp.int32)
    live_slots = positions[None, :] < lengths[:, None]
    masked = jnp.where(live_slots, score, jnp.float32(-1e30))
    rank_peak = jnp.max(masked, axis=1)
    rank_norm = rank_peak + jnp.log(
        jnp.sum(
            jnp.where(live_slots, jnp.exp(masked - rank_peak[:, None]), jnp.float32(0.0)), axis=1
        )
    )
    total_items = item_rows * device_count
    section = jnp.where(
        live_slots,
        score - rank_norm[:, None] + gen_logit - log_norm[:, None] + math.log(total_items),
        jnp.float32(0.0),
    )
    chosen = jnp.sum(
        jnp.where(positions[None, :] == logged_slot[:, None], section, jnp.float32(0.0)), axis=1
    )
    log_weight = (
        chosen
        + jnp.log(lengths.astype(jnp.float32))
        - jnp.log(logging_prop.astype(jnp.float32) / 1024.0)
    )
    return (section, log_weight)


def solution(mesh):
    in_specs = (
        P(("dp", "item"), None),
        P(("dp", "item"), None),
        P(("dp", "item"), None),
        P(("dp", "item"), None),
        P(("dp", "item")),
        P(("dp", "item")),
        P(("dp", "item")),
        P(),
        P(),
        P(),
    )
    out_specs = (P(("dp", "item"), None), P(("dp", "item")))
    return jax.shard_map(body, mesh=mesh, in_specs=in_specs, out_specs=out_specs, check_vma=False)
```

profile of v0, /device:TPU:0, one launch (start us, length us, event | category | flops | bytes accessed | tf_op | source)
XLA Modules:
  0.0 184.3 jit_solution(8159638173040724396)
XLA Ops:
  0.6 0.8 and_select_fusion
  1.4 0.7 add_select_fusion
  2.6 0.7 compare_select_fusion.1
  3.4 4.5 %scatter_custom_fusion = s32[1536]{0:T(1024)S(1)} fusion(s32[1024]{0:T(1024)S(1)} %bitcast.83, s32[1024]{0:T(1024)} %bitcast.81, s32[]{:T(128)} %constant.87.clone.1), kind=kCustom, calls=%fused_computation.53 | custom fusion | bytes 6656 | tf_op jit(solution)/shard_map/scatter | solution.py:72
  8.0 7.9 %all_to_all.20 = s32[4,1,384]{2,1,0:T(1,128)S(1)} all-to-all(s32[4,1,384]{2,1,0:T(1,128)S(1)} %reshape.234), channel_id=1, replica_groups=mesh['dp'=4,'item'=8] {'dp'}, dimensions={0} | all-to-all | bytes 12288 | tf_op jit(solution)/shard_map/all_to_all | solution.py:76
  17.2 0.7 reshape.236
  17.8 5.8 %all-to-all-start.1 = ((s32[8,1,192]{2,1,0:T(1,128)}), s32[8,1,192]{2,1,0:T(1,128)S(1)}, u32[]{:S(2)}, u32[]{:S(2)}) async-start(s32[8,1,192]{2,1,0:T(1,128)} %reshape.236), calls=%async_computation.1 | async-start | bytes 16384 | tf_op jit(solution)/shard_map/all_to_all | solution.py:75
  23.7 66.8 %all-gather.2 = bf16[32,1,256]{2,1,0:T(2,128)(2,1)S(1)} all-gather(bf16[1,1,256]{2,1,0:T(2,128)(2,1)} %bitcast.85), channel_id=1, replica_groups=mesh['dp'=4,'item'=8] {'dp','item'}, dimensions={0}, use_global_device_ids=true | all-gather | bytes 16896 | tf_op jit(solution)/shard_map/all_gather | solution.py:41
  91.3 5.9 %gather_fusion = bf16[1536,256]{1,0:T(8,128)(2,1)} fusion(bf16[2048,256]{1,0:T(8,128)(2,1)} %param.15, s32[2048]{0:T(1024)S(1)} %pad_clamp_fusion), kind=kCustom, calls=%fused_computation | custom fusion | bytes 1579008 | tf_op jit(solution)/shard_map/gather | solution.py:84
  97.2 3.5 %all-to-all-start.2 = ((bf16[4,8,48,256]{3,2,1,0:T(8,128)(2,1)}), bf16[4,8,48,256]{3,2,1,0:T(8,128)(2,1)S(1)}, u32[]{:S(2)}, u32[]{:S(2)}) async-start(bf16[4,8,48,256]{3,2,1,0:T(8,128)(2,1)} %bitcast.8), calls=%async_computation.2 | async-start | bytes 1572864 | tf_op jit(solution)/shard_map/all_to_all | solution.py:84
  100.7 6.0 %while.31 = (s32[]{:T(128)}, f32[32]{0:T(128)S(1)}, f32[32]{0:T(128)S(1)}, bf16[4,512,256]{2,1,0:T(8,128)(2,1)}, bf16[32,256]{1,0:T(8,128)(2,1)S(1)}, /*index=5*/s32[]{:T(128)}, s32[]{:T(128)}) while((s32[]{:T(128)}, f32[32]{0:T(128)S(1)}, f32[32]{0:T(128)S(1)}, bf16[4,512,256]{2,1,0:T(8,128)(2,1)}, bf16[32,256]{1,0:T(8,128)(2,1)S(1)}, ...), condition=%wide.region_7.8_spmd.clone, body=%wide.region_4.7_spmd.clone.sunk | while | flops 8437923 | bytes 411864 | solution.py:61
  100.7 1.2 fusion.42
  102.2 1.2 fusion.42
  103.7 1.2 fusion.42
  105.2 1.2 fusion.42
  107.2 37.0 %all-reduce.2 = (f32[1024]{0:T(1024)S(1)}, f32[1024]{0:T(1024)S(1)}) all-reduce(f32[1024]{0:T(1024)S(1)} %dynamic-update-slice, f32[1024]{0:T(1024)S(1)} %dynamic-update-slice.1), channel_id=2, replica_groups=mesh['dp'=4,'item'=8] {'dp','item'}, use_global_device_ids=true, to_apply=%add | all-reduce | flops 2048 | bytes 16384
  144.3 1.0 copy.24
  145.2 6.1 %all-to-all-start.3 = ((bf16[4,8,48,256]{3,2,0,1:T(8,128)(2,1)}), bf16[4,8,48,256]{3,2,0,1:T(8,128)(2,1)S(1)}, u32[]{:S(2)}, u32[]{:S(2)}) async-start(bf16[4,8,48,256]{3,2,0,1:T(8,128)(2,1)} %copy.24), calls=%async_computation.3 | async-start | bytes 1572864 | tf_op jit(solution)/shard_map/all_to_all | solution.py:83
  151.3 1.4 while.30
  155.6 15.6 %all-to-all-done.3 = bf16[4,8,48,256]{3,2,0,1:T(8,128)(2,1)S(1)} async-done(((bf16[4,8,48,256]{3,2,0,1:T(8,128)(2,1)}), bf16[4,8,48,256]{3,2,0,1:T(8,128)(2,1)S(1)}, u32[]{:S(2)}, u32[]{:S(2)}) %all-to-all-start.3) | async-done | bytes 786464 | tf_op jit(solution)/shard_map/all_to_all | solution.py:83
  171.3 3.9 %gather_fusion.1 = bf16[1024,256]{1,0:T(8,128)(2,1)S(1)} fusion(bf16[1536,256]{1,0:T(8,128)(2,1)S(1)} %bitcast.74, s32[1024]{0:T(1024)S(1)} %broadcast_clamp_fusion), kind=kCustom, calls=%fused_computation.1 | custom fusion | bytes 1052672 | tf_op jit(solution)/shard_map/gather | solution.py:90
  175.5 1.4 multiply_convert_fusion
  177.9 1.3 select_reduce_fusion.1
  180.6 1.9 %select_reduce_fusion = (f32[]{:T(128)}, f32[1024]{0:T(1024)}) fusion(s32[]{:T(128)} %bitcast.72, f32[]{:T(128)} %bitcast.15, f32[1024]{0:T(1024)S(1)} %bitcast.82, f32[1024]{0:T(1024)S(1)} %bitcast.78, f32[]{:T(128)S(6)} %add.144, s32[]{:T(128)} %bitcast.71), kind=kLoop, calls=%fused_computation.48 | loop fusion | flops 9215 | bytes 12308 | tf_op jit(solution)/shard_map/reduce_sum | solution.py:122
  (92 shorter events, 7.3 us)
Async XLA Ops:
  0.6 174.8 %copy-start = (bf16[512,512]{1,0:T(8,128)(2,1)S(1)}, bf16[512,512]{1,0:T(8,128)(2,1)}, u32[]{:S(2)}) copy-start(bf16[512,512]{1,0:T(8,128)(2,1)} %param.22) | copy-start | bytes 1572868
  17.8 72.6 %all-to-all-start.1 = ((s32[8,1,192]{2,1,0:T(1,128)}), s32[8,1,192]{2,1,0:T(1,128)S(1)}, u32[]{:S(2)}, u32[]{:S(2)}) async-start(s32[8,1,192]{2,1,0:T(1,128)} %reshape.236), calls=%async_computation.1 | async-start | bytes 16384 | tf_op jit(solution)/shard_map/all_to_all | solution.py:75
  97.2 47.1 %all-to-all-start.2 = ((bf16[4,8,48,256]{3,2,1,0:T(8,128)(2,1)}), bf16[4,8,48,256]{3,2,1,0:T(8,128)(2,1)S(1)}, u32[]{:S(2)}, u32[]{:S(2)}) async-start(bf16[4,8,48,256]{3,2,1,0:T(8,128)(2,1)} %bitcast.8), calls=%async_computation.2 | async-start | bytes 1572864 | tf_op jit(solution)/shard_map/all_to_all | solution.py:84
  145.2 7.5 %copy-start.4 = (bf16[512]{0:T(512)(128)(2,1)S(1)}, bf16[512]{0:T(512)(128)(2,1)}, u32[]{:S(2)}) copy-start(bf16[512]{0:T(512)(128)(2,1)} %param.23) | copy-start | bytes 3076
  145.2 10.2 %copy-start.1 = (bf16[768,512]{1,0:T(8,128)(2,1)S(1)}, bf16[768,512]{1,0:T(8,128)(2,1)}, u32[]{:S(2)}) copy-start(bf16[768,512]{1,0:T(8,128)(2,1)} %param.21) | copy-start | bytes 2359300
  145.2 10.2 %copy-start.3 = (bf16[1,512]{1,0:T(2,128)(2,1)S(1)}, bf16[1,512]{1,0:T(2,128)(2,1)}, u32[]{:S(2)}) copy-start(bf16[1,512]{1,0:T(2,128)(2,1)} %param.16) | copy-start | bytes 3076
  145.2 25.9 %all-to-all-start.3 = ((bf16[4,8,48,256]{3,2,0,1:T(8,128)(2,1)}), bf16[4,8,48,256]{3,2,0,1:T(8,128)(2,1)S(1)}, u32[]{:S(2)}, u32[]{:S(2)}) async-start(bf16[4,8,48,256]{3,2,0,1:T(8,128)(2,1)} %copy.24), calls=%async_computation.3 | async-start | bytes 1572864 | tf_op jit(solution)/shard_map/all_to_all | solution.py:83
  171.2 4.0 %copy-start.2 = (bf16[1,256]{1,0:T(2,128)(2,1)S(1)}, bf16[1,256]{1,0:T(2,128)(2,1)}, u32[]{:S(2)}) copy-start(bf16[1,256]{1,0:T(2,128)(2,1)} %param.14) | copy-start | bytes 1540
where the time goes:
time: 185 us; the launch traced here: 184 us
  blocking collectives  112 us (61%)
  local copies, waits for them, and re-layouts  18.2 us (10%)
  waiting for transfers between devices  15.6 us (8%)
  starting transfers between devices  15.4 us (8%)
  other arithmetic  9.64 us (5%)
  matrix products  7.17 us (4%)
  between operations  6.05 us (3%)
    all_gather x1, blocking collectives, body(): gathered = lax.all_gather(query, ('dp', 'item'), axis=0, tiled=True)  66.8 us
    unnamed x1, blocking collectives  37 us
    all_to_all x1, waiting for transfers between devices, body(): lax.all_to_all(lax.all_to_all(item_table[local_index], 'dp', split_axis=0...  15.6 us
    all_to_all x1, blocking collectives, body(): lax.all_to_all(outgoing, 'dp', split_axis=0, concat_axis=0, tiled=True)  7.87 us
    all_to_all x1, starting transfers between devices, body(): lax.all_to_all(lax.all_to_all(item_table[local_index], 'dp', split_axis=0...  6.09 us
    gather x1, local copies, waits for them, and re-layouts, body(): item_table[local_index]  5.85 us
    all_to_all x1, starting transfers between devices, body(): lax.all_to_all(lax.all_to_all(outgoing, 'dp', split_axis=0, concat_axis=0...  5.81 us
    dot_general x4, matrix products, sweep(): lax.dot_general(gathered, slab_rows, (((1,), (1,)), ((), ())), preferred_...  4.97 us
  transfers between devices with their start and end apart: 3, of which 1 were waited for; matrix products, arithmetic and copies ran while one was open for 4% of the time, Pallas kernels for 0%

commit v1 on v0

--- a/solution.py
+++ b/solution.py
@@ -80,13 +80,10 @@
         tiled=True,
     )
     local_index = jnp.clip(asked_ids - first_item, 0, item_rows - 1)
-    fetched = lax.all_to_all(
-        lax.all_to_all(item_table[local_index], "dp", split_axis=0, concat_axis=0, tiled=True),
-        "item",
-        split_axis=1,
-        concat_axis=1,
-        tiled=True,
-    )
+    own = lax.all_to_all(item_table[local_index], "dp", split_axis=0, concat_axis=0, tiled=True)
+    pieces = jnp.split(own, lax.axis_size("item"), axis=1)
+    arrived = lax.all_to_all(jnp.stack(pieces), "item", 0, 0)
+    fetched = jnp.concatenate(arrived, axis=1)
     cand_rows = fetched.reshape(device_count * capacity, width)[bucket]
     rows_by_context = cand_rows.reshape(own_count, slot_count, width)
     gen_logit = jnp.einsum("cd,ckd->ck", query, rows_by_context, preferred_element_type=jnp.float32)

time: 185 us -> 189 us (1.022)
  local copies, waits for them, and re-layouts: 18.2 us -> 22.3 us
    unnamed x18 -> x25, local copies, waits for them, and re-layouts: 1.42 us -> 5.91 us
where the time goes in v1:
time: 189 us; the launch traced here: 188 us
  blocking collectives  112 us (59%)
  local copies, waits for them, and re-layouts  22.3 us (12%)
  waiting for transfers between devices  15.6 us (8%)
  starting transfers between devices  15.3 us (8%)
  other arithmetic  9.64 us (5%)
  matrix products  7.17 us (4%)
  between operations  6.06 us (3%)
    all_gather x1, blocking collectives, body(): gathered = lax.all_gather(query, ('dp', 'item'), axis=0, tiled=True)  66.8 us
    unnamed x1, blocking collectives  37 us
    all_to_all x1, waiting for transfers between devices, body(): arrived = lax.all_to_all(jnp.stack(pieces), 'item', 0, 0)  15.6 us
    all_to_all x1, blocking collectives, body(): lax.all_to_all(outgoing, 'dp', split_axis=0, concat_axis=0, tiled=True)  7.87 us
    all_to_all x1, starting transfers between devices, body(): arrived = lax.all_to_all(jnp.stack(pieces), 'item', 0, 0)  5.96 us
    unnamed x25, local copies, waits for them, and re-layouts  5.91 us
    gather x1, local copies, waits for them, and re-layouts, body(): item_table[local_index]  5.85 us
    all_to_all x1, starting transfers between devices, body(): lax.all_to_all(lax.all_to_all(outgoing, 'dp', split_axis=0, concat_axis=0...  5.81 us
  transfers between devices with their start and end apart: 3, of which 1 were waited for; matrix products, arithmetic and copies ran while one was open for 4% of the time, Pallas kernels for 0%

profile of v1, /device:TPU:0, one launch (start us, length us, event | category | flops | bytes accessed | tf_op | source)
XLA Modules:
  0.0 188.4 jit_solution(11264271317777659092)
XLA Ops:
  0.6 0.8 and_select_fusion
  1.4 0.7 add_select_fusion
  2.6 0.7 compare_select_fusion.1
  3.4 4.5 %scatter_custom_fusion = s32[1536]{0:T(1024)S(1)} fusion(s32[1024]{0:T(1024)S(1)} %bitcast.131, s32[1024]{0:T(1024)} %bitcast.129, s32[]{:T(128)} %constant.87.clone.1), kind=kCustom, calls=%fused_computation.69 | custom fusion | bytes 6656 | tf_op jit(solution)/shard_map/scatter | solution.py:72
  8.0 7.9 %all_to_all.20 = s32[4,1,384]{2,1,0:T(1,128)S(1)} all-to-all(s32[4,1,384]{2,1,0:T(1,128)S(1)} %reshape.234), channel_id=1, replica_groups=mesh['dp'=4,'item'=8] {'dp'}, dimensions={0} | all-to-all | bytes 12288 | tf_op jit(solution)/shard_map/all_to_all | solution.py:76
  17.2 0.7 reshape.236
  17.8 5.8 %all-to-all-start.1 = ((s32[8,1,192]{2,1,0:T(1,128)}), s32[8,1,192]{2,1,0:T(1,128)S(1)}, u32[]{:S(2)}, u32[]{:S(2)}) async-start(s32[8,1,192]{2,1,0:T(1,128)} %reshape.236), calls=%async_computation.1 | async-start | bytes 16384 | tf_op jit(solution)/shard_map/all_to_all | solution.py:75
  23.7 66.8 %all-gather.2 = bf16[32,1,256]{2,1,0:T(2,128)(2,1)S(1)} all-gather(bf16[1,1,256]{2,1,0:T(2,128)(2,1)} %bitcast.133), channel_id=1, replica_groups=mesh['dp'=4,'item'=8] {'dp','item'}, dimensions={0}, use_global_device_ids=true | all-gather | bytes 16896 | tf_op jit(solution)/shard_map/all_gather | solution.py:41
  90.5 0.7 reduce.9
  91.3 5.9 %gather_fusion = bf16[1536,256]{1,0:T(8,128)(2,1)} fusion(bf16[2048,256]{1,0:T(8,128)(2,1)} %param.15, s32[2048]{0:T(1024)S(1)} %pad_clamp_fusion), kind=kCustom, calls=%fused_computation | custom fusion | bytes 1579008 | tf_op jit(solution)/shard_map/gather | solution.py:83
  97.2 3.5 %all-to-all-start.2 = ((bf16[4,8,48,256]{3,2,1,0:T(8,128)(2,1)}), bf16[4,8,48,256]{3,2,1,0:T(8,128)(2,1)S(1)}, u32[]{:S(2)}, u32[]{:S(2)}) async-start(bf16[4,8,48,256]{3,2,1,0:T(8,128)(2,1)} %bitcast.8), calls=%async_computation.2 | async-start | bytes 1572864 | tf_op jit(solution)/shard_map/all_to_all | solution.py:83
  100.7 6.0 %while.31 = (s32[]{:T(128)}, f32[32]{0:T(128)S(1)}, f32[32]{0:T(128)S(1)}, bf16[4,512,256]{2,1,0:T(8,128)(2,1)}, bf16[32,256]{1,0:T(8,128)(2,1)S(1)}, /*index=5*/s32[]{:T(128)}, s32[]{:T(128)}) while((s32[]{:T(128)}, f32[32]{0:T(128)S(1)}, f32[32]{0:T(128)S(1)}, bf16[4,512,256]{2,1,0:T(8,128)(2,1)}, bf16[32,256]{1,0:T(8,128)(2,1)S(1)}, ...), condition=%wide.region_7.8_spmd.clone, body=%wide.region_4.7_spmd.clone.sunk | while | flops 8437923 | bytes 411864 | solution.py:61
  100.7 1.2 fusion.50
  102.2 1.2 fusion.50
  103.7 1.2 fusion.50
  105.2 1.2 fusion.50
  107.2 37.0 %all-reduce.2 = (f32[1024]{0:T(1024)S(1)}, f32[1024]{0:T(1024)S(1)}) all-reduce(f32[1024]{0:T(1024)S(1)} %dynamic-update-slice, f32[1024]{0:T(1024)S(1)} %dynamic-update-slice.1), channel_id=2, replica_groups=mesh['dp'=4,'item'=8] {'dp','item'}, use_global_device_ids=true, to_apply=%add | all-reduce | flops 2048 | bytes 16384
  149.4 6.0 %all-to-all-start.3 = ((bf16[8,4,1,48,256]{4,3,1,2,0:T(8,128)(2,1)}), bf16[8,4,1,48,256]{4,3,1,2,0:T(8,128)(2,1)S(1)}, u32[]{:S(2)}, u32[]{:S(2)}) async-start(bf16[8,4,1,48,256]{4,3,1,2,0:T(8,128)(2,1)} %fusion.17), calls=%async_computation.3 | async-start | bytes 1572864 | tf_op jit(solution)/shard_map/all_to_all | solution.py:85
  155.4 1.4 while.30
  159.6 15.6 %all-to-all-done.3 = bf16[8,4,1,48,256]{4,3,1,2,0:T(8,128)(2,1)S(1)} async-done(((bf16[8,4,1,48,256]{4,3,1,2,0:T(8,128)(2,1)}), bf16[8,4,1,48,256]{4,3,1,2,0:T(8,128)(2,1)S(1)}, u32[]{:S(2)}, u32[]{:S(2)}) %all-to-all-start.3) | async-done | bytes 786464 | tf_op jit(solution)/shard_map/all_to_all | solution.py:85
  175.3 3.9 %gather_fusion.1 = bf16[1024,256]{1,0:T(8,128)(2,1)S(1)} fusion(bf16[1536,256]{1,0:T(8,128)(2,1)S(1)} %bitcast.121, s32[1024]{0:T(1024)S(1)} %broadcast_clamp_fusion), kind=kCustom, calls=%fused_computation.1 | custom fusion | bytes 1052672 | tf_op jit(solution)/shard_map/gather | solution.py:87
  179.5 1.4 multiply_convert_fusion
  181.9 1.3 select_reduce_fusion.1
  184.6 1.9 %select_reduce_fusion = (f32[]{:T(128)}, f32[1024]{0:T(1024)}) fusion(s32[]{:T(128)} %bitcast.119, f32[]{:T(128)} %bitcast.24, f32[1024]{0:T(1024)S(1)} %bitcast.130, f32[1024]{0:T(1024)S(1)} %bitcast.126, f32[]{:T(128)S(6)} %add.144, s32[]{:T(128)} %bitcast.118), kind=kLoop, calls=%fused_computation.64 | loop fusion | flops 9215 | bytes 12308 | tf_op jit(solution)/shard_map/reduce_sum | solution.py:119
  (99 shorter events, 11.7 us)
Async XLA Ops:
  0.6 178.9 %copy-start = (bf16[512,512]{1,0:T(8,128)(2,1)S(1)}, bf16[512,512]{1,0:T(8,128)(2,1)}, u32[]{:S(2)}) copy-start(bf16[512,512]{1,0:T(8,128)(2,1)} %param.22) | copy-start | bytes 1572868
  17.8 72.6 %all-to-all-start.1 = ((s32[8,1,192]{2,1,0:T(1,128)}), s32[8,1,192]{2,1,0:T(1,128)S(1)}, u32[]{:S(2)}, u32[]{:S(2)}) async-start(s32[8,1,192]{2,1,0:T(1,128)} %reshape.236), calls=%async_computation.1 | async-start | bytes 16384 | tf_op jit(solution)/shard_map/all_to_all | solution.py:75
  97.2 47.1 %all-to-all-start.2 = ((bf16[4,8,48,256]{3,2,1,0:T(8,128)(2,1)}), bf16[4,8,48,256]{3,2,1,0:T(8,128)(2,1)S(1)}, u32[]{:S(2)}, u32[]{:S(2)}) async-start(bf16[4,8,48,256]{3,2,1,0:T(8,128)(2,1)} %bitcast.8), calls=%async_computation.2 | async-start | bytes 1572864 | tf_op jit(solution)/shard_map/all_to_all | solution.py:83
  148.8 8.0 %copy-start.4 = (bf16[512]{0:T(512)(128)(2,1)S(1)}, bf16[512]{0:T(512)(128)(2,1)}, u32[]{:S(2)}) copy-start(bf16[512]{0:T(512)(128)(2,1)} %param.23) | copy-start | bytes 3076
  148.8 10.7 %copy-start.1 = (bf16[768,512]{1,0:T(8,128)(2,1)S(1)}, bf16[768,512]{1,0:T(8,128)(2,1)}, u32[]{:S(2)}) copy-start(bf16[768,512]{1,0:T(8,128)(2,1)} %param.21) | copy-start | bytes 2359300
  148.8 10.7 %copy-start.3 = (bf16[1,512]{1,0:T(2,128)(2,1)S(1)}, bf16[1,512]{1,0:T(2,128)(2,1)}, u32[]{:S(2)}) copy-start(bf16[1,512]{1,0:T(2,128)(2,1)} %param.16) | copy-start | bytes 3076
  149.4 25.8 %all-to-all-start.3 = ((bf16[8,4,1,48,256]{4,3,1,2,0:T(8,128)(2,1)}), bf16[8,4,1,48,256]{4,3,1,2,0:T(8,128)(2,1)S(1)}, u32[]{:S(2)}, u32[]{:S(2)}) async-start(bf16[8,4,1,48,256]{4,3,1,2,0:T(8,128)(2,1)} %fusion.17), calls=%async_computation.3 | async-start | bytes 1572864 | tf_op jit(solution)/shard_map/all_to_all | solution.py:85
  175.3 4.0 %copy-start.2 = (bf16[1,256]{1,0:T(2,128)(2,1)S(1)}, bf16[1,256]{1,0:T(2,128)(2,1)}, u32[]{:S(2)}) copy-start(bf16[1,256]{1,0:T(2,128)(2,1)} %param.14) | copy-start | bytes 1540
